TPU v7x, 256 devices: a whole 4x4x8 slice. The times are simulated.
256 devices in a mesh: grp: 8 (over z), slab: 32 (over y, x, core).
Axes of the slice: x: 4, y: 4, z: 8, core: 2. Of those that a mesh axis runs over, the one named last changes fastest.
Arguments:
- spectra: bfloat16 [131072, 2048], P(('grp', 'slab')), may hold values from -6 to 6
- ctf_sq: bfloat16 [131072, 1024], P(('grp', 'slab')), may hold values from 0.049804688 to 1
- dest: int32 [131072, 1], P(('grp', 'slab')), may hold values from 0 to 31; in each aligned block of 512 rows (0 to 511, 512 to 1023, ...) at most 32 rows name the same one
- block: int32 [131072], P(('grp', 'slab')), may hold values from 0 to 63
- pattern: int32 [131072], P(('grp', 'slab')), may hold values from 0 to 63
- pattern_table: bfloat16 [64, 8], replicated, may hold values from 0.049804688 to 1
- tau: float32 [1024], replicated, may hold values from 0.5 to 4
Outputs:
- image: float32 [2, 16, 1024, 1024], P(None, 'grp', None, 'slab')
Inputs may be any that keep to these rules, and one draw needn't show every extreme that they name: `dest`: among the rows of one device at most 32 name the same slab; in some device's rows one slab is named by exactly 32.
All inputs are finite; a program needn't handle non-finite values.
Results may differ from a plain program's by a relative error of at most 0.0003.
Values may be sent and summed in bfloat16 or wider, within the bound.
A program may use at most 192 MiB of HBM per device.

v0:
```python
import math
import jax
import jax.numpy as jnp
from jax import lax
from jax.sharding import PartitionSpec as P

KZ_DEV = 32
YWIN = 16
NBLK = 64


def dft_tables(length):
    indices = jnp.arange(length, dtype=jnp.int32)
    product = indices[:, None] * indices[None, :] % length
    angles = product.astype(jnp.float32) * (2.0 * math.pi / length)
    return (jnp.cos(angles), jnp.sin(angles))


def inverse_kz(filtered, cosine, sine):
    real_part = filtered[:, :, 0, :]
    imag_part = filtered[:, :, 1, :]
    scaling = 1.0 / math.sqrt(cosine.shape[0])
    highest = lax.Precision.HIGHEST
    out_real = jnp.einsum("zk,ykx->yzx", cosine, real_part, precision=highest) - jnp.einsum(
        "zk,ykx->yzx", sine, imag_part, precision=highest
    )
    out_imag = jnp.einsum("zk,ykx->yzx", sine, real_part, precision=highest) + jnp.einsum(
        "zk,ykx->yzx", cosine, imag_part, precision=highest
    )
    return jnp.stack([out_real * scaling, out_imag * scaling])


def on_device(spectra, ctf_sq, dest, block, pattern, pattern_table, tau):
    slab_count = lax.axis_size("slab")
    rows_here = spectra.shape[0]
    kx_width = ctf_sq.shape[1]
    spread = pattern_table.shape[1]
    capacity = max(2, 2 * rows_here // slab_count)
    slot_total = slab_count * capacity
    slab_ids = jnp.arange(slab_count, dtype=jnp.int32)
    matches = (dest == slab_ids[None, :]).astype(jnp.int32)
    earlier = jnp.cumsum(matches, axis=0) - matches
    position = jnp.sum(earlier * matches, axis=1)
    target = dest[:, 0] * capacity + position
    pattern_ids = jnp.arange(pattern_table.shape[0], dtype=jnp.int32)
    pattern_onehot = (pattern[:, None] == pattern_ids[None, :]).astype(jnp.bfloat16)
    row_weights = jnp.dot(pattern_onehot, pattern_table, preferred_element_type=jnp.float32).astype(
        jnp.bfloat16
    )
    block_label = (block + 1).astype(jnp.float32).astype(jnp.bfloat16)[:, None]
    send_spec = jnp.zeros((slot_total, 2 * kx_width), jnp.bfloat16).at[target].set(spectra)
    send_ctf = jnp.zeros((slot_total, kx_width), jnp.bfloat16).at[target].set(ctf_sq)
    send_weights = jnp.zeros((slot_total, spread), jnp.bfloat16).at[target].set(row_weights)
    send_label = jnp.zeros((slot_total, 1), jnp.bfloat16).at[target].set(block_label)
    got_spec, got_ctf, got_weights, got_label = (
        lax.all_to_all(send_spec, "slab", split_axis=0, concat_axis=0, tiled=True),
        lax.all_to_all(send_ctf, "slab", split_axis=0, concat_axis=0, tiled=True),
        lax.all_to_all(send_weights, "slab", split_axis=0, concat_axis=0, tiled=True),
        lax.all_to_all(send_label, "slab", split_axis=0, concat_axis=0, tiled=True),
    )
    block_ids = jnp.arange(1, NBLK + 1, dtype=jnp.int32).astype(jnp.float32)
    block_match = (got_label.astype(jnp.float32) == block_ids[None, :]).astype(jnp.bfloat16)
    spreader = (block_match[:, :, None] * got_weights[:, None, :]).reshape(
        slot_total, NBLK * spread
    )
    contract = (((0,), (0,)), ((), ()))
    cosine, sine = dft_tables(KZ_DEV * slab_count)
    column_width = kx_width // slab_count
    data_sum = lax.dot_general(spreader, got_spec, contract, preferred_element_type=jnp.float32)
    weight_sum = lax.dot_general(spreader, got_ctf, contract, preferred_element_type=jnp.float32)
    data_sum = data_sum.reshape(YWIN, KZ_DEV, 2, kx_width)
    weight_sum = weight_sum.reshape(YWIN, KZ_DEV, 1, kx_width)
    volume = jnp.concatenate([data_sum, weight_sum], axis=2)
    columns_all = lax.all_to_all(volume, "slab", split_axis=3, concat_axis=1, tiled=True)
    summed = lax.psum_scatter(columns_all, "grp", scatter_dimension=0, tiled=True)
    tau_part = lax.dynamic_slice_in_dim(tau, lax.axis_index("slab") * column_width, column_width, 0)
    filtered = summed[:, :, 0:2, :] / (summed[:, :, 2:3, :] + tau_part[None, None, None, :])
    image = inverse_kz(filtered, cosine, sine)
    return image


def solution(mesh):
    in_specs = (
        P(("grp", "slab"), None),
        P(("grp", "slab"), None),
        P(("grp", "slab"), None),
        P(("grp", "slab")),
        P(("grp", "slab")),
        P(),
        P(),
    )
    out_specs = P(None, "grp", None, "slab")
    return jax.shard_map(
        on_device, mesh=mesh, in_specs=in_specs, out_specs=out_specs, check_vma=False
    )
```

profile of v0, /device:TPU:1, one launch (start us, length us, event | category | flops | bytes accessed | tf_op | source)
XLA Modules:
  0.0 599.7 jit_solution(15534419843716490866)
XLA Ops:
  7.2 1.2 reduce-window.6
  10.8 3.8 scatter_custom_fusion
  15.3 8.6 %all-to-all-start = ((bf16[32,32,1]{1,2,0:T(2,128)(2,1)}), bf16[32,32,1]{1,2,0:T(2,128)(2,1)S(1)}, u32[]{:S(2)}, u32[]{:S(2)}) async-start(bf16[32,32,1]{1,2,0:T(2,128)(2,1)} %all_to_all.55), calls=%async_computation | async-start | bytes 32768 | tf_op jit(solution)/shard_map/all_to_all | solution.py:59
  23.9 0.9 convolution_convert_fusion
  25.0 1.8 scatter_custom_fusion.1
  27.7 3.1 all-to-all-done
  30.8 4.2 all-to-all-start.1
  35.1 4.8 scatter_custom_fusion.3
  39.9 2.1 all-to-all-done.1
  42.0 5.7 all-to-all-start.3
  47.7 7.3 %scatter_custom_fusion.2 = bf16[1024,2048]{1,0:T(8,128)(2,1)} fusion(s32[512]{0:T(512)S(1)} %bitcast.129, bf16[512,2048]{1,0:T(8,128)(2,1)} %param.7, bf16[]{:T(256)} %constant.12.clone.1), kind=kCustom, calls=%fused_computation.24 | custom fusion | bytes 4194816 | tf_op jit(solution)/shard_map/scatter | solution.py:51
  55.0 21.3 %all-to-all-done.3 = bf16[32,32,1024]{2,1,0:T(8,128)(2,1)S(1)} async-done(((bf16[32,32,1024]{2,1,0:T(8,128)(2,1)}), bf16[32,32,1024]{2,1,0:T(8,128)(2,1)S(1)}, u32[]{:S(2)}, u32[]{:S(2)}) %all-to-all-start.3) | async-done | bytes 2097184 | tf_op jit(solution)/shard_map/all_to_all | solution.py:57
  76.2 6.1 %all-to-all-start.2 = ((bf16[32,32,2048]{2,1,0:T(8,128)(2,1)}), bf16[32,32,2048]{2,1,0:T(8,128)(2,1)}, u32[]{:S(2)}, u32[]{:S(2)}) async-start(bf16[32,32,2048]{2,1,0:T(8,128)(2,1)} %bitcast.115), calls=%async_computation.2 | async-start | bytes 8388608 | tf_op jit(solution)/shard_map/all_to_all | solution.py:56
  83.0 2.7 convolution_bitcast_fusion
  85.7 47.4 %all-to-all-done.2 = bf16[32,32,2048]{2,1,0:T(8,128)(2,1)} async-done(((bf16[32,32,2048]{2,1,0:T(8,128)(2,1)}), bf16[32,32,2048]{2,1,0:T(8,128)(2,1)}, u32[]{:S(2)}, u32[]{:S(2)}) %all-to-all-start.2) | async-done | bytes 4194336 | tf_op jit(solution)/shard_map/all_to_all | solution.py:56
  133.0 6.4 %copy.34 = bf16[2048,1024]{1,0:T(8,128)(2,1)} copy(bf16[2048,1024]{0,1:T(8,128)(2,1)} %bitcast.13) | data formatting | bytes 8388608 | tf_op jit(solution)/shard_map/dot_general | solution.py:69
  139.4 4.7 fusion.68
  144.1 3.3 pad_maximum_fusion
  147.4 18.1 %copy.35 = f32[16,32,3,1024]{1,0,2,3:T(8,128)} copy(f32[16,32,3,1024]{3,1,2,0:T(8,128)} %pad_maximum_fusion) | data formatting | bytes 12582912 | tf_op jit(solution)/shard_map/concatenate | solution.py:73
  165.5 27.1 %reshape.150 = f32[32,1,49152]{2,1,0:T(1,128)} reshape(f32[1024,3,16,32]{3,2,1,0:T(8,128)} %bitcast.114) | data formatting | bytes 12582912
  192.7 82.1 %all_to_all.61 = f32[32,1,49152]{2,1,0:T(1,128)} all-to-all(f32[32,1,49152]{2,1,0:T(1,128)} %reshape.150), channel_id=1, replica_groups=mesh['grp'=8,'slab'=32] {'slab'}, dimensions={0} | all-to-all | bytes 12582912 | tf_op jit(solution)/shard_map/all_to_all | solution.py:74
  275.3 19.9 %reduce.6 = f32[32,49152]{1,0:T(8,128)} reduce(f32[32,1,49152]{2,1,0:T(1,128)} %all_to_all.61, f32[]{:T(128)} %broadcast.112), dimensions={1}, to_apply=%all_to_all.51.reduce_sub_computation | reduce | bytes 12582916 | tf_op jit(solution)/shard_map/all_to_all | solution.py:74
  295.2 24.4 %reshape.151 = f32[1024,3,16,32]{3,2,1,0:T(8,128)} reshape(f32[32,49152]{1,0:T(8,128)} %reduce.6) | data formatting | bytes 12582912
  319.6 24.7 %copy.36 = f32[16,32,32,3,32]{2,1,4,0,3:T(8,128)} copy(f32[16,32,32,3,32]{2,0,3,4,1:T(8,128)} %bitcast.113) | data formatting | bytes 12582912 | tf_op jit(solution)/shard_map/all_to_all | solution.py:74
  344.3 20.1 %all_to_all.54 = f32[16,1024,3,32]{1,3,0,2:T(8,128)} reshape(f32[16,32,32,3,32]{2,1,4,0,3:T(8,128)} %copy.36) | data formatting | bytes 12582912 | tf_op jit(solution)/shard_map/all_to_all | solution.py:74
  366.4 146.4 %all-reduce.3.cloned.1.call-done = f32[16,1024,3,32]{1,3,0,2:T(8,128)} async-done(((f32[16,1024,3,32]{1,3,0,2:T(8,128)}), f32[16,1024,3,32]{1,3,0,2:T(8,128)}) %all-reduce.3.cloned.1.call-update) | async-done | bytes 6291472
  512.8 1.0 fusion.42
  513.9 1.1 dynamic-slice_divide_fusion
  515.0 19.1 %fusion.5 = f32[2,32,1024]{2,1,0:T(8,128)S(1)} fusion(f32[2,1024,2,32]{1,3,0,2:T(8,128)S(1)} %dynamic-slice_divide_fusion), kind=kOutput, calls=%fused_computation.13 | convolution fusion | flops 819986432 | bytes 524288 | tf_op jit(solution)/shard_map/zk,ykx->yzx/dot_general | solution.py:24
  534.1 19.4 %fusion.3 = f32[2,32,1024]{2,1,0:T(8,128)S(1)} fusion(f32[2,1024,2,32]{1,3,0,2:T(8,128)S(1)} %dynamic-slice_divide_fusion), kind=kOutput, calls=%fused_computation.11 | convolution fusion | flops 819986432 | bytes 524288 | tf_op jit(solution)/shard_map/zk,ykx->yzx/dot_general | solution.py:27
  553.5 19.0 %fusion.37 = f32[1,2,1024,32]{2,3,1,0:T(8,128)S(1)} fusion(f32[2,32,1024]{2,1,0:T(8,128)S(1)} %fusion.5, f32[2,1024,2,32]{1,3,0,2:T(8,128)S(1)} %dynamic-slice_divide_fusion), kind=kOutput, calls=%fused_computation.32 | convolution fusion | flops 820117504 | bytes 786432 | tf_op jit(solution)/shard_map/zk,ykx->yzx/dot_general | solution.py:24
  572.5 19.3 %fusion.31 = f32[1,2,1024,32]{2,3,1,0:T(8,128)S(1)} fusion(f32[2,32,1024]{2,1,0:T(8,128)S(1)} %fusion.3, f32[2,1024,2,32]{1,3,0,2:T(8,128)S(1)} %dynamic-slice_divide_fusion), kind=kOutput, calls=%fused_computation.30 | convolution fusion | flops 820117504 | bytes 786432 | tf_op jit(solution)/shard_map/zk,ykx->yzx/dot_general | solution.py:27
  (33 shorter events, 8.2 us)
Async XLA Ops:
  6.5 17.3 %copy-start = (bf16[64,8]{0,1:T(8,128)(2,1)S(1)}, bf16[64,8]{0,1:T(8,128)(2,1)}, u32[]{:S(2)}) copy-start(bf16[64,8]{0,1:T(8,128)(2,1)} %param.12) | copy-start | bytes 3076
  15.3 15.6 %all-to-all-start = ((bf16[32,32,1]{1,2,0:T(2,128)(2,1)}), bf16[32,32,1]{1,2,0:T(2,128)(2,1)S(1)}, u32[]{:S(2)}, u32[]{:S(2)}) async-start(bf16[32,32,1]{1,2,0:T(2,128)(2,1)} %all_to_all.55), calls=%async_computation | async-start | bytes 32768 | tf_op jit(solution)/shard_map/all_to_all | solution.py:59
  30.8 11.1 %all-to-all-start.1 = ((bf16[32,2,128]{2,1,0:T(2,128)(2,1)}), bf16[32,2,128]{2,1,0:T(2,128)(2,1)S(1)}, u32[]{:S(2)}, u32[]{:S(2)}) async-start(bf16[32,2,128]{2,1,0:T(2,128)(2,1)} %reshape.148), calls=%async_computation.1 | async-start | bytes 32768 | tf_op jit(solution)/shard_map/all_to_all | solution.py:58
  42.0 34.3 %all-to-all-start.3 = ((bf16[32,32,1024]{2,1,0:T(8,128)(2,1)}), bf16[32,32,1024]{2,1,0:T(8,128)(2,1)S(1)}, u32[]{:S(2)}, u32[]{:S(2)}) async-start(bf16[32,32,1024]{2,1,0:T(8,128)(2,1)} %bitcast.18), calls=%async_computation.3 | async-start | bytes 4194304 | tf_op jit(solution)/shard_map/all_to_all | solution.py:57
  76.2 56.8 %all-to-all-start.2 = ((bf16[32,32,2048]{2,1,0:T(8,128)(2,1)}), bf16[32,32,2048]{2,1,0:T(8,128)(2,1)}, u32[]{:S(2)}, u32[]{:S(2)}) async-start(bf16[32,32,2048]{2,1,0:T(8,128)(2,1)} %bitcast.115), calls=%async_computation.2 | async-start | bytes 8388608 | tf_op jit(solution)/shard_map/all_to_all | solution.py:56
  82.3 430.5 %all-reduce.3.cloned.1.call-start = ((), (), s32[]{:S(2)}) async-start(), calls=%async_computation.5 | async-start | bytes 12582912
  139.4 4.7 copy-start.2
  364.4 0.8 copy-start.3
  572.5 20.2 %copy-start.1 = (bf16[64,8]{0,1:T(8,128)(2,1)S(1)}, bf16[64,8]{0,1:T(8,128)(2,1)}, u32[]{:S(2)}) copy-start(bf16[64,8]{0,1:T(8,128)(2,1)} %param.12) | copy-start | bytes 3076
Sparse Core Ops, SparseCore 0:
  364.5 148.2 all-reduce.2
where the time goes:
time: 609 us; the launch traced here: 600 us
  waiting for transfers between devices  220 us (36%)
  local copies, waits for them, and re-layouts  143 us (23%)
  matrix products  85.1 us (14%)
  blocking collectives  82.1 us (13%)
  other arithmetic  30.5 us (5%)
  starting transfers between devices  24.7 us (4%)
  between operations  14.4 us (2%)
    unnamed x2, waiting for transfers between devices  146 us
    all_to_all x1, blocking collectives, on_device(): lax.all_to_all(volume, 'slab', split_axis=3, concat_axis=1, tiled=True)  82.1 us
    unnamed x13, local copies, waits for them, and re-layouts  52.9 us
    all_to_all x1, waiting for transfers between devices, on_device(): lax.all_to_all(send_spec, 'slab', split_axis=0, concat_axis=0, tiled=True)  47.4 us
    all_to_all x3, local copies, waits for them, and re-layouts, on_device(): lax.all_to_all(volume, 'slab', split_axis=3, concat_axis=1, tiled=True)  45.3 us
    all_to_all x1, waiting for transfers between devices, on_device(): lax.all_to_all(send_ctf, 'slab', split_axis=0, concat_axis=0, tiled=True)  21.3 us
    all_to_all x1, other arithmetic, on_device(): lax.all_to_all(volume, 'slab', split_axis=3, concat_axis=1, tiled=True)  19.9 us
    dot_general x1, matrix products, inverse_kz(): jnp.einsum('zk,ykx->yzx', sine, real_part, precision=highest)  19.4 us
  transfers between devices with their start and end apart: 5, of which 5 were waited for; matrix products, arithmetic and copies ran while one was open for 3% of the time, Pallas kernels for 0%

commit v1 on v0

--- a/solution.py
+++ b/solution.py
@@ -71,7 +71,15 @@
     data_sum = data_sum.reshape(YWIN, KZ_DEV, 2, kx_width)
     weight_sum = weight_sum.reshape(YWIN, KZ_DEV, 1, kx_width)
     volume = jnp.concatenate([data_sum, weight_sum], axis=2)
-    columns_all = lax.all_to_all(volume, "slab", split_axis=3, concat_axis=1, tiled=True)
+    columns_all = jnp.concatenate(
+        lax.all_to_all(
+            jnp.stack(jnp.split(volume, lax.psum(1, axis_name="slab"), 3)),
+            split_axis=0,
+            concat_axis=0,
+            axis_name="slab",
+        ),
+        axis=1,
+    )
     summed = lax.psum_scatter(columns_all, "grp", scatter_dimension=0, tiled=True)
     tau_part = lax.dynamic_slice_in_dim(tau, lax.axis_index("slab") * column_width, column_width, 0)
     filtered = summed[:, :, 0:2, :] / (summed[:, :, 2:3, :] + tau_part[None, None, None, :])

time: 609 us -> 624 us (1.025)
  local copies, waits for them, and re-layouts: 143 us -> 153 us
    reshape x0 -> x3, local copies, waits for them, and re-layouts: none -> 65.2 us  [on_device(): jnp.concatenate(lax.all_to_all(jnp.stack(jnp.split(volume, lax.psum(1, ax...]
    all_to_all x3 -> x1, local copies, waits for them, and re-layouts: 45.3 us -> 0.51 us  [on_device(): lax.all_to_all(jnp.stack(jnp.split(volume, lax.psum(1, axis_name='slab'),...]
    concatenate x1 -> x0, local copies, waits for them, and re-layouts: 18.1 us -> none  [on_device(): volume = jnp.concatenate([data_sum, weight_sum], axis=2)]
    unnamed x13 -> x15, local copies, waits for them, and re-layouts: 52.9 us -> 61.4 us
    unnamed x0 -> x31, other arithmetic: none -> 7.07 us
where the time goes in v1:
time: 624 us; the launch traced here: 614 us
  waiting for transfers between devices  220 us (35%)
  local copies, waits for them, and re-layouts  153 us (25%)
  matrix products  85.1 us (14%)
  blocking collectives  81.8 us (13%)
  other arithmetic  34.5 us (6%)
  starting transfers between devices  24.8 us (4%)
  between operations  14.6 us (2%)
    unnamed x2, waiting for transfers between devices  146 us
    all_to_all x1, blocking collectives, on_device(): lax.all_to_all(jnp.stack(jnp.split(volume, lax.psum(1, axis_name='slab'),...  81.8 us
    reshape x3, local copies, waits for them, and re-layouts, on_device(): jnp.concatenate(lax.all_to_all(jnp.stack(jnp.split(volume, lax.psum(1, ax...  65.2 us
    unnamed x15, local copies, waits for them, and re-layouts  61.4 us
    all_to_all x1, waiting for transfers between devices, on_device(): lax.all_to_all(send_spec, 'slab', split_axis=0, concat_axis=0, tiled=True)  47.1 us
    all_to_all x1, waiting for transfers between devices, on_device(): lax.all_to_all(send_ctf, 'slab', split_axis=0, concat_axis=0, tiled=True)  21.3 us
    all_to_all x1, other arithmetic, on_device(): lax.all_to_all(jnp.stack(jnp.split(volume, lax.psum(1, axis_name='slab'),...  19.8 us
    dot_general x1, matrix products, inverse_kz(): jnp.einsum('zk,ykx->yzx', sine, imag_part, precision=highest)  19.3 us
  transfers between devices with their start and end apart: 5, of which 5 were waited for; matrix products, arithmetic and copies ran while one was open for 3% of the time, Pallas kernels for 0%

profile of v1, /device:TPU:1, one launch (start us, length us, event | category | flops | bytes accessed | tf_op | source)
XLA Modules:
  0.0 614.2 jit_solution(8456903932820175969)
XLA Ops:
  7.2 1.2 reduce-window.6
  10.8 3.8 scatter_custom_fusion
  15.3 8.6 %all-to-all-start = ((bf16[32,32,1]{1,2,0:T(2,128)(2,1)}), bf16[32,32,1]{1,2,0:T(2,128)(2,1)S(1)}, u32[]{:S(2)}, u32[]{:S(2)}) async-start(bf16[32,32,1]{1,2,0:T(2,128)(2,1)} %all_to_all.42), calls=%async_computation | async-start | bytes 32768 | tf_op jit(solution)/shard_map/all_to_all | solution.py:59
  23.9 0.9 convolution_convert_fusion
  25.0 1.8 scatter_custom_fusion.1
  27.7 3.1 all-to-all-done
  30.8 4.2 all-to-all-start.1
  35.1 4.8 scatter_custom_fusion.3
  39.9 2.1 all-to-all-done.1
  42.0 5.9 all-to-all-start.3
  47.9 7.2 %scatter_custom_fusion.2 = bf16[1024,2048]{1,0:T(8,128)(2,1)} fusion(s32[512]{0:T(512)S(1)} %bitcast.256, bf16[512,2048]{1,0:T(8,128)(2,1)} %param.7, bf16[]{:T(256)} %constant.12.clone.1), kind=kCustom, calls=%fused_computation.85 | custom fusion | bytes 4194816 | tf_op jit(solution)/shard_map/scatter | solution.py:51
  55.1 21.3 %all-to-all-done.3 = bf16[32,32,1024]{2,1,0:T(8,128)(2,1)S(1)} async-done(((bf16[32,32,1024]{2,1,0:T(8,128)(2,1)}), bf16[32,32,1024]{2,1,0:T(8,128)(2,1)S(1)}, u32[]{:S(2)}, u32[]{:S(2)}) %all-to-all-start.3) | async-done | bytes 2097184 | tf_op jit(solution)/shard_map/all_to_all | solution.py:57
  76.4 6.1 all-to-all-start.2
  83.2 2.9 convolution_bitcast_fusion
  86.0 47.1 %all-to-all-done.2 = bf16[32,32,2048]{2,1,0:T(8,128)(2,1)} async-done(((bf16[32,32,2048]{2,1,0:T(8,128)(2,1)}), bf16[32,32,2048]{2,1,0:T(8,128)(2,1)}, u32[]{:S(2)}, u32[]{:S(2)}) %all-to-all-start.2) | async-done | bytes 4194336 | tf_op jit(solution)/shard_map/all_to_all | solution.py:56
  133.2 6.4 %copy.26 = bf16[2048,1024]{1,0:T(8,128)(2,1)} copy(bf16[2048,1024]{0,1:T(8,128)(2,1)} %bitcast.13) | data formatting | bytes 8388608 | tf_op jit(solution)/shard_map/dot_general | solution.py:69
  139.6 4.6 fusion.163
  151.6 8.3 %copy-done.2 = f32[32,16,32,3,32]{4,2,3,1,0:T(8,128)} copy-done((f32[32,16,32,3,32]{4,2,3,1,0:T(8,128)}, f32[32,16,32,3,32]{4,2,3,1,0:T(8,128)S(1)}, u32[]{:S(2)}) %copy-start.2) | copy-done | bytes 6291480
  159.9 27.1 %reshape.159 = f32[32,1,49152]{2,1,0:T(1,128)} reshape(f32[32,16,3,32,32]{4,3,2,1,0:T(8,128)} %bitcast.241) | data formatting | bytes 12582912
  187.0 81.8 %all_to_all.48 = f32[32,1,49152]{2,1,0:T(1,128)} all-to-all(f32[32,1,49152]{2,1,0:T(1,128)} %reshape.159), channel_id=1, replica_groups=mesh['grp'=8,'slab'=32] {'slab'}, dimensions={0} | all-to-all | bytes 12582912 | tf_op jit(solution)/shard_map/all_to_all | solution.py:75
  269.3 19.8 %reduce.6 = f32[32,49152]{1,0:T(8,128)} reduce(f32[32,1,49152]{2,1,0:T(1,128)} %all_to_all.48, f32[]{:T(128)} %broadcast.112), dimensions={1}, to_apply=%all_to_all.41.reduce_sub_computation | reduce | bytes 12582916 | tf_op jit(solution)/shard_map/all_to_all | solution.py:75
  289.1 24.5 %reshape.160 = f32[32,16,3,32,32]{4,3,2,1,0:T(8,128)} reshape(f32[32,49152]{1,0:T(8,128)} %reduce.6) | data formatting | bytes 12582912
  313.6 18.0 %bitcast_bitcast_fusion.1 = f32[16,32,32,3,32]{4,2,3,0,1:T(8,128)} fusion(f32[32,16,3,32,32]{4,3,2,1,0:T(8,128)} %reshape.160), kind=kLoop, calls=%fused_computation.236 | loop fusion | bytes 12582912 | tf_op jit(solution)/shard_map/reshape | solution.py:74
  331.7 27.1 %copy.30 = f32[16,32,32,3,32]{2,1,4,0,3:T(8,128)} copy(f32[16,32,32,3,32]{4,2,3,0,1:T(8,128)} %bitcast_bitcast_fusion.1) | data formatting | bytes 12582912 | tf_op jit(solution)/shard_map/reshape | solution.py:74
  358.7 20.1 %reshape.137 = f32[16,1024,3,32]{1,3,0,2:T(8,128)} reshape(f32[16,32,32,3,32]{2,1,4,0,3:T(8,128)} %copy.30) | data formatting | bytes 12582912 | tf_op jit(solution)/shard_map/reshape | solution.py:74
  380.9 146.4 %all-reduce.3.cloned.1.call-done = f32[16,1024,3,32]{1,3,0,2:T(8,128)} async-done(((f32[16,1024,3,32]{1,3,0,2:T(8,128)}), f32[16,1024,3,32]{1,3,0,2:T(8,128)}) %all-reduce.3.cloned.1.call-update) | async-done | bytes 6291472
  527.3 1.0 fusion.137
  528.3 1.1 dynamic-slice_divide_fusion
  529.4 19.3 %fusion.5 = f32[2,32,1024]{2,1,0:T(8,128)S(1)} fusion(f32[2,1024,2,32]{1,3,0,2:T(8,128)S(1)} %dynamic-slice_divide_fusion), kind=kOutput, calls=%fused_computation.74 | convolution fusion | flops 819986432 | bytes 524288 | tf_op jit(solution)/shard_map/zk,ykx->yzx/dot_general | solution.py:24
  548.7 19.2 %fusion.3 = f32[2,32,1024]{2,1,0:T(8,128)S(1)} fusion(f32[2,1024,2,32]{1,3,0,2:T(8,128)S(1)} %dynamic-slice_divide_fusion), kind=kOutput, calls=%fused_computation.72 | convolution fusion | flops 819986432 | bytes 524288 | tf_op jit(solution)/shard_map/zk,ykx->yzx/dot_general | solution.py:27
  568.0 19.1 %fusion.37 = f32[1,2,1024,32]{2,3,1,0:T(8,128)S(1)} fusion(f32[2,32,1024]{2,1,0:T(8,128)S(1)} %fusion.5, f32[2,1024,2,32]{1,3,0,2:T(8,128)S(1)} %dynamic-slice_divide_fusion), kind=kOutput, calls=%fused_computation.93 | convolution fusion | flops 820117504 | bytes 786432 | tf_op jit(solution)/shard_map/zk,ykx->yzx/dot_general | solution.py:24
  587.2 19.1 %fusion.31 = f32[1,2,1024,32]{2,3,1,0:T(8,128)S(1)} fusion(f32[2,32,1024]{2,1,0:T(8,128)S(1)} %fusion.3, f32[2,1024,2,32]{1,3,0,2:T(8,128)S(1)} %dynamic-slice_divide_fusion), kind=kOutput, calls=%fused_computation.91 | convolution fusion | flops 820117504 | bytes 786432 | tf_op jit(solution)/shard_map/zk,ykx->yzx/dot_general | solution.py:27
  (66 shorter events, 15.5 us)
Async XLA Ops:
  6.5 17.3 %copy-start = (bf16[64,8]{0,1:T(8,128)(2,1)S(1)}, bf16[64,8]{0,1:T(8,128)(2,1)}, u32[]{:S(2)}) copy-start(bf16[64,8]{0,1:T(8,128)(2,1)} %param.12) | copy-start | bytes 3076
  15.3 15.6 %all-to-all-start = ((bf16[32,32,1]{1,2,0:T(2,128)(2,1)}), bf16[32,32,1]{1,2,0:T(2,128)(2,1)S(1)}, u32[]{:S(2)}, u32[]{:S(2)}) async-start(bf16[32,32,1]{1,2,0:T(2,128)(2,1)} %all_to_all.42), calls=%async_computation | async-start | bytes 32768 | tf_op jit(solution)/shard_map/all_to_all | solution.py:59
  30.8 11.1 %all-to-all-start.1 = ((bf16[32,2,128]{2,1,0:T(2,128)(2,1)}), bf16[32,2,128]{2,1,0:T(2,128)(2,1)S(1)}, u32[]{:S(2)}, u32[]{:S(2)}) async-start(bf16[32,2,128]{2,1,0:T(2,128)(2,1)} %reshape.157), calls=%async_computation.1 | async-start | bytes 32768 | tf_op jit(solution)/shard_map/all_to_all | solution.py:58
  42.0 34.4 %all-to-all-start.3 = ((bf16[32,32,1024]{2,1,0:T(8,128)(2,1)}), bf16[32,32,1024]{2,1,0:T(8,128)(2,1)S(1)}, u32[]{:S(2)}, u32[]{:S(2)}) async-start(bf16[32,32,1024]{2,1,0:T(8,128)(2,1)} %bitcast.18), calls=%async_computation.3 | async-start | bytes 4194304 | tf_op jit(solution)/shard_map/all_to_all | solution.py:57
  76.4 6.8 %copy-start.3 = (bf16[32,32,1024]{2,1,0:T(8,128)(2,1)}, bf16[32,32,1024]{2,1,0:T(8,128)(2,1)S(1)}, u32[]{:S(2)}) copy-start(bf16[32,32,1024]{2,1,0:T(8,128)(2,1)S(1)} %all-to-all-done.3) | copy-start | bytes 6291460
  76.4 56.8 %all-to-all-start.2 = ((bf16[32,32,2048]{2,1,0:T(8,128)(2,1)}), bf16[32,32,2048]{2,1,0:T(8,128)(2,1)}, u32[]{:S(2)}, u32[]{:S(2)}) async-start(bf16[32,32,2048]{2,1,0:T(8,128)(2,1)} %bitcast.242), calls=%async_computation.2 | async-start | bytes 8388608 | tf_op jit(solution)/shard_map/all_to_all | solution.py:56
  82.5 444.8 %all-reduce.3.cloned.1.call-start = ((), (), s32[]{:S(2)}) async-start(), calls=%async_computation.5 | async-start | bytes 12582912
  151.6 8.3 %copy-start.2 = (f32[32,16,32,3,32]{4,2,3,1,0:T(8,128)}, f32[32,16,32,3,32]{4,2,3,1,0:T(8,128)S(1)}, u32[]{:S(2)}) copy-start(f32[32,16,32,3,32]{4,2,3,1,0:T(8,128)S(1)} %fusion.136) | copy-start | bytes 18874372
  378.8 0.8 copy-start.4
  568.0 39.1 %copy-start.1 = (bf16[64,8]{0,1:T(8,128)(2,1)S(1)}, bf16[64,8]{0,1:T(8,128)(2,1)}, u32[]{:S(2)}) copy-start(bf16[64,8]{0,1:T(8,128)(2,1)} %param.12) | copy-start | bytes 3076
Sparse Core Ops, SparseCore 0:
  379.0 148.2 all-reduce.2
